TPU v7x, 32 devices: a whole 2x2x4 slice. The times are simulated.
32 devices in a mesh: section: 4 (over y, x), tensor: 8 (over z, core).
Axes of the slice: x: 2, y: 2, z: 4, core: 2. Of those that a mesh axis runs over, the one named last changes fastest.
Arguments:
- hidden_last: bfloat16 [512, 6656], P(None, 'tensor'), may hold values from -6 to 6
- labels: int32 [512], replicated, may hold values from 0 to 31999
- head_weight: bfloat16 [6656, 32000], P(None, 'tensor'), may hold values from -0.21875 to 0.21875
- layer_inputs: bfloat16 [4, 512, 6656], P('section', None, 'tensor'), may hold values from -6 to 6
- weights: bfloat16 [4, 6656, 6656], P('section', 'tensor'), may hold values from -0.078125 to 0.078125
- row_state: float32 [4, 6656], P('section', 'tensor'), may hold values from 1.173753e-06 to 0.000498845
- col_state: float32 [4, 6656], P('section'), may hold values from 1e-08 to 1e-06
Outputs:
- loss: float32 [], replicated
- input_grads: bfloat16 [4, 512, 6656], P('section', None, 'tensor')
- new_weights: bfloat16 [4, 6656, 6656], P('section', 'tensor')
- new_row_state: float32 [4, 6656], P('section', 'tensor')
- new_col_state: float32 [4, 6656], P('section')
All inputs are finite; a program needn't handle non-finite values.
Results may differ from a plain program's by a relative error of at most 0.007.
Values may be sent and summed in bfloat16 or wider, within the bound.
A program may use at most 192 MiB of HBM per device.

v0:
```python
import jax
import jax.numpy as jnp
from jax import lax
from jax.sharding import PartitionSpec as P

decay_rate = 0.9
learn_rate = 0.3
tiny_term = 1e-30


def shifted(block, axis, distance):
    devices = range(lax.axis_size(axis))
    route = [(i - distance, i) for i in devices if i - distance in devices]
    return lax.ppermute(block, axis, route)


def body(hidden_last, labels, head_weight, layer_inputs, weights, row_state, col_state):
    section_count = lax.axis_size("section")
    section_index = lax.axis_index("section")
    all_rows = labels.shape[0]
    model_width = head_weight.shape[0]
    vocab_local = head_weight.shape[1]
    local_weight = weights[0]
    rows_local = local_weight.shape[0]
    saved_all = layer_inputs[0]
    columns = lax.axis_index("tensor") * vocab_local + lax.iota(jnp.int32, vocab_local)
    share_rows = all_rows // section_count
    row_start = section_index * share_rows
    hidden_rows = lax.dynamic_slice_in_dim(hidden_last, row_start, share_rows, 0)
    head_slice = head_weight
    logits = jnp.dot(
        lax.all_gather(hidden_rows, "tensor", axis=1, tiled=True),
        head_slice,
        preferred_element_type=jnp.float32,
    )
    exponent = jnp.exp(logits)
    label_hit = (
        lax.dynamic_slice_in_dim(labels, row_start, share_rows, 0)[:, None] == columns[None, :]
    )
    denominator, picked = lax.psum(
        (
            jnp.sum(exponent, axis=1),
            jnp.sum(jnp.where(label_hit, logits, jnp.zeros_like(logits)), axis=1),
        ),
        "tensor",
    )
    losses = jnp.log(denominator) - picked
    logit_grad = (
        (exponent / denominator[:, None] - label_hit.astype(jnp.float32)) / all_rows
    ).astype(jnp.bfloat16)
    head_slice = head_weight
    shares = lax.psum_scatter(
        lax.dot_general(
            head_slice, logit_grad, (((1,), (1,)), ((), ())), preferred_element_type=jnp.float32
        ),
        "tensor",
        scatter_dimension=0,
        tiled=True,
    )
    part_grad = shares.T.astype(jnp.bfloat16)
    part_loss = jnp.sum(losses)
    head_grad = lax.all_gather(part_grad, "section", axis=0, tiled=True)
    loss = lax.psum(part_loss, "section") / all_rows
    is_last = section_index == section_count - 1

    def layer_block(dy_rows, saved_rows):
        gathered = lax.all_gather(dy_rows, "tensor", axis=1, tiled=True)
        backward = lax.dot_general(
            gathered, local_weight, (((1,), (1,)), ((), ())), preferred_element_type=jnp.float32
        )
        product = lax.dot_general(
            saved_rows, gathered, (((0,), (0,)), ((), ())), preferred_element_type=jnp.float32
        )
        backward, piece_grad = (backward, product)
        input_grad = (dy_rows.astype(jnp.float32) + backward).astype(jnp.bfloat16)
        return (input_grad, piece_grad)

    start_grad = jnp.zeros((rows_local, model_width), jnp.float32)

    def advance_whole(step_index, loop_state):
        received, gradient, outputs = loop_state
        active = step_index == section_count - 1 - section_index
        dy_rows = jnp.where(is_last, head_grad, received)
        input_grad, piece_grad = layer_block(dy_rows, saved_all)
        gradient = gradient + jnp.where(active, piece_grad, jnp.zeros_like(piece_grad))
        outputs = jnp.where(active, input_grad, outputs)
        received = shifted(input_grad, "section", -1)
        return (received, gradient, outputs)

    loop_state = (
        jnp.zeros((all_rows, rows_local), jnp.bfloat16),
        start_grad,
        jnp.zeros((all_rows, rows_local), jnp.bfloat16),
    )
    loop_state = lax.fori_loop(0, section_count, advance_whole, loop_state)
    gradient = loop_state[1]
    outputs = loop_state[2]
    weight_float = local_weight.astype(jnp.float32)
    squares = gradient * gradient + tiny_term
    row_new = decay_rate * row_state[0] + (1.0 - decay_rate) * jnp.mean(squares, axis=1)
    col_part = jnp.sum(squares, axis=0)
    entries = float(model_width * model_width)
    col_sum, row_total, weight_total = lax.psum(
        (col_part, jnp.sum(row_new), jnp.sum(weight_float * weight_float)), "tensor"
    )
    col_new = decay_rate * col_state[0] + (1.0 - decay_rate) * (col_sum / model_width)
    update = gradient / jnp.sqrt(row_new[:, None] * col_new[None, :] / row_total)
    update_total = lax.psum(jnp.sum(update * update), "tensor")
    factor = (
        learn_rate
        * jnp.sqrt(weight_total / entries)
        / jnp.maximum(1.0, jnp.sqrt(update_total / entries))
    )
    new_weight = (weight_float - factor * update).astype(jnp.bfloat16)
    return (loss, outputs[None], new_weight[None], row_new[None], col_new[None])


def solution(mesh):
    return jax.shard_map(
        body,
        mesh=mesh,
        in_specs=(
            P(None, "tensor"),
            P(),
            P(None, "tensor"),
            P("section", None, "tensor"),
            P("section", "tensor", None),
            P("section", "tensor"),
            P("section", None),
        ),
        out_specs=(
            P(),
            P("section", None, "tensor"),
            P("section", "tensor", None),
            P("section", "tensor"),
            P("section", None),
        ),
        check_vma=False,
    )
```

profile of v0, /device:TPU:0, one launch (start us, length us, event | category | flops | bytes accessed | tf_op | source)
XLA Modules:
  0.0 680.5 jit_solution(17623979021237377767)
XLA Ops:
  9.9 29.1 %all-gather.3.cloned.1.call-done = bf16[128,6656]{0,1:T(8,128)(2,1)} async-done(((bf16[128,832]{0,1:T(8,128)(2,1)}), bf16[128,6656]{0,1:T(8,128)(2,1)}) %all-gather.3.cloned.1.call-update) | async-done | bytes 1703952 | tf_op jit(solution)/shard_map/all_gather | solution.py:32
  39.0 22.1 %exponential_reduce_fusion = (f32[128]{0:T(128)S(1)}, f32[128]{0:T(128)}, f32[128,4000]{0,1:T(8,128)S(1)}) fusion(s32[4000]{0:T(1024)S(1)} %iota_add_fusion, s32[128]{0:T(128)S(1)} %dynamic_slice.7, bf16[6656,4000]{0,1:T(8,128)(2,1)} %param.11, bf16[128,6656]{0,1:T(8,128)(2,1)} %all-gather.3.cloned.1.call-done), kind=kOutput, calls=%fused_computation.21 | convolution fusion | flops 6817792000 | bytes 57017472 | tf_op jit(solution)/shard_map/dot_general | solution.py:31
  61.0 15.1 %psum.49 = f32[128]{0:T(128)S(1)} all-reduce(f32[128]{0:T(128)S(1)} %get-tuple-element.270), channel_id=1, replica_groups=mesh['section'=4,'tensor'=8] {'tensor'}, use_global_device_ids=true, to_apply=%region_1.2 | all-reduce | flops 128 | bytes 1024 | tf_op jit(solution)/shard_map/psum | solution.py:40
  76.2 20.9 %convolution_bitcast_fusion = f32[6656,128]{0,1:T(8,128)} fusion(bf16[6656,4000]{0,1:T(8,128)(2,1)} %param.11, f32[128,4000]{0,1:T(8,128)S(1)} %get-tuple-element.300, f32[128]{0:T(128)S(1)} %psum.49, s32[128]{0:T(128)S(1)} %dynamic_slice.7, s32[4000]{0:T(1024)S(1)} %iota_add_fusion), kind=kOutput, calls=%fused_computation.14 | convolution fusion | flops 6818816000 | bytes 58720896 | tf_op jit(solution)/shard_map/dot_general | solution.py:53
  97.1 5.1 copy.16
  104.1 10.8 %fusion = f32[]{:T(128)} fusion(bf16[1,832,6656]{2,1,0:T(8,128)(2,1)} %param.13), kind=kLoop, calls=%fused_computation.6 | loop fusion | flops 16613375 | bytes 11075588 | tf_op jit(solution)/shard_map/reduce_sum | solution.py:104
  114.9 28.1 %reduce-scatter.4.cloned.1.call-done = f32[832,128]{1,0:T(8,128)} async-done(((f32[6656,128]{1,0:T(8,128)}), f32[832,128]{1,0:T(8,128)}) %reduce-scatter.4.cloned.1.call-update) | async-done | bytes 426000
  144.1 12.6 %all_gather.16 = bf16[512,832]{1,0:T(8,128)(2,1)S(1)} all-gather(bf16[128,832]{1,0:T(8,128)(2,1)S(1)} %bitcast.35), channel_id=1, replica_groups=mesh['section'=4,'tensor'=8] {'section'}, dimensions={0}, use_global_device_ids=true | all-gather | bytes 1064960 | tf_op jit(solution)/shard_map/all_gather | solution.py:62
  157.3 420.9 %while.20 = (s32[]{:T(128)}, bf16[512,832]{0,1:T(8,128)(2,1)S(1)}, f32[832,6656]{1,0:T(8,128)}, bf16[512,832]{0,1:T(8,128)(2,1)}, pred[]{:T(512)}, /*index=5*/bf...) while((s32[]{:T(128)}, bf16[512,832]{0,1:T(8,128)(2,1)S(1)}, ...), condition=%wide.region_8.9_spmd.clone, body=%wide.region_7.8_spmd.clone.sunk | while | flops 11360567296 | bytes 102236368 | solution.py:95
  158.4 70.2 %all-gather.5.cloned.1.call-done = bf16[512,6656]{0,1:T(8,128)(2,1)} async-done(((bf16[512,832]{0,1:T(8,128)(2,1)}), bf16[512,6656]{0,1:T(8,128)(2,1)}) %all-gather.5.cloned.1.call-update) | async-done | bytes 6815760 | tf_op jit(solution)/shard_map/while/body/eval_jaxpr/all_gather | solution.py:67
  228.6 11.6 %select_select_fusion.2 = (bf16[512,832]{0,1:T(8,128)(2,1)}, bf16[512,832]{0,1:T(8,128)(2,1)S(1)}) fusion(bf16[512,832]{0,1:T(8,128)(2,1)} %get-tuple-element.374, pred[]{:T(512)S(6)} %compare.3, pred[]{:T(512)S(6)} %eq.52, bf16[832,6656]{1,0:T(8,128)(2,1)} %get-tuple-element.388, bf16[512,6656]{0,1:T(8,128)(2,1)} %all-gather.5.cloned.1.call-done, ...), kind=kOutput, calls=%fused_computation.2.clone.1 | convolution fusion | flops 5672828928 | bytes 21299202 | tf_op jit(solution)/shard_map/while/body/eval_jaxpr/dot_general | solution.py:68
  240.1 1.3 collective-permute-start
  241.4 12.6 %bitcast_add_fusion.2 = f32[832,6656]{1,0:T(8,128)} fusion(f32[832,6656]{1,0:T(8,128)} %get-tuple-element.373, bf16[512,6656]{0,1:T(8,128)(2,1)} %all-gather.5.cloned.1.call-done, bf16[512,832]{1,0:T(8,128)(2,1)S(1)} %get-tuple-element.390, pred[]{:T(512)S(6)} %compare.3, pred[]{:T(512)S(6)} %eq.52), kind=kOutput, calls=%fused_computation.clone.1 | convolution fusion | flops 5687312384 | bytes 51970048 | tf_op jit(solution)/shard_map/while/body/eval_jaxpr/dot_general | solution.py:71
  254.1 9.1 %collective-permute-done = bf16[512,832]{0,1:T(8,128)(2,1)S(1)} collective-permute-done((bf16[512,832]{0,1:T(8,128)(2,1)S(1)}, bf16[512,832]{0,1:T(8,128)(2,1)S(1)}, u32[]{:S(2)}, u32[]{:S(2)}) %collective-permute-start) | collective-permute-done | bytes 852000 | tf_op jit(solution)/shard_map/while/body/eval_jaxpr/ppermute | solution.py:14
  264.1 69.3 %all-gather.5.cloned.1.call-done = bf16[512,6656]{0,1:T(8,128)(2,1)} async-done(((bf16[512,832]{0,1:T(8,128)(2,1)}), bf16[512,6656]{0,1:T(8,128)(2,1)}) %all-gather.5.cloned.1.call-update) | async-done | bytes 6815760 | tf_op jit(solution)/shard_map/while/body/eval_jaxpr/all_gather | solution.py:67
  333.5 11.7 %select_select_fusion.2 = (bf16[512,832]{0,1:T(8,128)(2,1)}, bf16[512,832]{0,1:T(8,128)(2,1)S(1)}) fusion(bf16[512,832]{0,1:T(8,128)(2,1)} %get-tuple-element.374, pred[]{:T(512)S(6)} %compare.3, pred[]{:T(512)S(6)} %eq.52, bf16[832,6656]{1,0:T(8,128)(2,1)} %get-tuple-element.388, bf16[512,6656]{0,1:T(8,128)(2,1)} %all-gather.5.cloned.1.call-done, ...), kind=kOutput, calls=%fused_computation.2.clone.1 | convolution fusion | flops 5672828928 | bytes 21299202 | tf_op jit(solution)/shard_map/while/body/eval_jaxpr/dot_general | solution.py:68
  346.5 16.7 %bitcast_add_fusion.2 = f32[832,6656]{1,0:T(8,128)} fusion(f32[832,6656]{1,0:T(8,128)} %get-tuple-element.373, bf16[512,6656]{0,1:T(8,128)(2,1)} %all-gather.5.cloned.1.call-done, bf16[512,832]{1,0:T(8,128)(2,1)S(1)} %get-tuple-element.390, pred[]{:T(512)S(6)} %compare.3, pred[]{:T(512)S(6)} %eq.52), kind=kOutput, calls=%fused_computation.clone.1 | convolution fusion | flops 5687312384 | bytes 51970048 | tf_op jit(solution)/shard_map/while/body/eval_jaxpr/dot_general | solution.py:71
  363.1 5.0 collective-permute-done
  369.2 69.3 %all-gather.5.cloned.1.call-done = bf16[512,6656]{0,1:T(8,128)(2,1)} async-done(((bf16[512,832]{0,1:T(8,128)(2,1)}), bf16[512,6656]{0,1:T(8,128)(2,1)}) %all-gather.5.cloned.1.call-update) | async-done | bytes 6815760 | tf_op jit(solution)/shard_map/while/body/eval_jaxpr/all_gather | solution.py:67
  438.5 11.7 %select_select_fusion.2 = (bf16[512,832]{0,1:T(8,128)(2,1)}, bf16[512,832]{0,1:T(8,128)(2,1)S(1)}) fusion(bf16[512,832]{0,1:T(8,128)(2,1)} %get-tuple-element.374, pred[]{:T(512)S(6)} %compare.3, pred[]{:T(512)S(6)} %eq.52, bf16[832,6656]{1,0:T(8,128)(2,1)} %get-tuple-element.388, bf16[512,6656]{0,1:T(8,128)(2,1)} %all-gather.5.cloned.1.call-done, ...), kind=kOutput, calls=%fused_computation.2.clone.1 | convolution fusion | flops 5672828928 | bytes 21299202 | tf_op jit(solution)/shard_map/while/body/eval_jaxpr/dot_general | solution.py:68
  451.5 16.7 %bitcast_add_fusion.2 = f32[832,6656]{1,0:T(8,128)} fusion(f32[832,6656]{1,0:T(8,128)} %get-tuple-element.373, bf16[512,6656]{0,1:T(8,128)(2,1)} %all-gather.5.cloned.1.call-done, bf16[512,832]{1,0:T(8,128)(2,1)S(1)} %get-tuple-element.390, pred[]{:T(512)S(6)} %compare.3, pred[]{:T(512)S(6)} %eq.52), kind=kOutput, calls=%fused_computation.clone.1 | convolution fusion | flops 5687312384 | bytes 51970048 | tf_op jit(solution)/shard_map/while/body/eval_jaxpr/dot_general | solution.py:71
  468.2 5.0 collective-permute-done
  474.2 69.3 %all-gather.5.cloned.1.call-done = bf16[512,6656]{0,1:T(8,128)(2,1)} async-done(((bf16[512,832]{0,1:T(8,128)(2,1)}), bf16[512,6656]{0,1:T(8,128)(2,1)}) %all-gather.5.cloned.1.call-update) | async-done | bytes 6815760 | tf_op jit(solution)/shard_map/while/body/eval_jaxpr/all_gather | solution.py:67
  543.6 11.7 %select_select_fusion.2 = (bf16[512,832]{0,1:T(8,128)(2,1)}, bf16[512,832]{0,1:T(8,128)(2,1)S(1)}) fusion(bf16[512,832]{0,1:T(8,128)(2,1)} %get-tuple-element.374, pred[]{:T(512)S(6)} %compare.3, pred[]{:T(512)S(6)} %eq.52, bf16[832,6656]{1,0:T(8,128)(2,1)} %get-tuple-element.388, bf16[512,6656]{0,1:T(8,128)(2,1)} %all-gather.5.cloned.1.call-done, ...), kind=kOutput, calls=%fused_computation.2.clone.1 | convolution fusion | flops 5672828928 | bytes 21299202 | tf_op jit(solution)/shard_map/while/body/eval_jaxpr/dot_general | solution.py:68
  556.6 16.7 %bitcast_add_fusion.2 = f32[832,6656]{1,0:T(8,128)} fusion(f32[832,6656]{1,0:T(8,128)} %get-tuple-element.373, bf16[512,6656]{0,1:T(8,128)(2,1)} %all-gather.5.cloned.1.call-done, bf16[512,832]{1,0:T(8,128)(2,1)S(1)} %get-tuple-element.390, pred[]{:T(512)S(6)} %compare.3, pred[]{:T(512)S(6)} %eq.52), kind=kOutput, calls=%fused_computation.clone.1 | convolution fusion | flops 5687312384 | bytes 51970048 | tf_op jit(solution)/shard_map/while/body/eval_jaxpr/dot_general | solution.py:71
  573.2 5.0 collective-permute-done
  578.3 9.7 %fusion.2 = (f32[6656]{0:T(1024)S(1)}, f32[832]{0:T(1024)S(1)}) fusion(f32[832,6656]{1,0:T(8,128)} %get-tuple-element.219), kind=kLoop, calls=%fused_computation.11 | loop fusion | flops 22143680 | bytes 22181120 | tf_op jit(solution)/shard_map/reduce_sum | solution.py:101
  588.6 26.0 %all-reduce.1 = (f32[]{:T(128)}, f32[6656]{0:T(1024)S(1)}) all-reduce(f32[]{:T(128)} %get-tuple-element.295, f32[6656]{0:T(1024)S(1)} %get-tuple-element.268), channel_id=1, replica_groups=mesh['section'=4,'tensor'=8] {'tensor'}, use_global_device_ids=true, to_apply=%region_15.16 | all-reduce | flops 6657 | bytes 53256 | tf_op jit(solution)/shard_map/psum | solution.py:103
  614.6 11.9 %multiply_reduce_fusion = f32[]{:T(128)} fusion(f32[832,6656]{1,0:T(8,128)} %get-tuple-element.219, f32[]{:T(128)} %get-tuple-element.293, f32[6656]{0:T(1024)S(1)} %multiply_add_fusion.1, f32[832]{0:T(1024)S(1)} %get-tuple-element.296), kind=kLoop, calls=%fused_computation.8 | loop fusion | flops 27688960 | bytes 22181128 | tf_op jit(solution)/shard_map/reduce_sum | solution.py:108
  626.5 14.2 %all-reduce = (f32[128]{0:T(128)S(1)}, f32[]{:T(128)}, f32[]{:T(128)}) all-reduce(f32[128]{0:T(128)S(1)} %copy-done.10, f32[]{:T(128)} %fusion, f32[]{:T(128)} %multiply_reduce_fusion), channel_id=1, replica_groups=mesh['section'=4,'tensor'=8] {'tensor'}, use_global_device_ids=true, to_apply=%region_3.4 | all-reduce | flops 130 | bytes 1040 | tf_op jit(solution)/shard_map/psum | solution.py:40
  642.2 17.4 %fusion.4 = bf16[1,832,6656]{2,1,0:T(8,128)(2,1)} fusion(f32[]{:T(128)S(6)} %div.49, bf16[1,832,6656]{2,1,0:T(8,128)(2,1)} %bitcast.33, f32[832,6656]{1,0:T(8,128)} %get-tuple-element.219, f32[]{:T(128)} %get-tuple-element.293, f32[6656]{0:T(1024)S(1)} %multiply_add_fusion.1, f32[832]{0:T(1024)S(1)} %get-tuple-element.296), kind=kLoop, calls=%fused_computation.13 | loop fusion | flops 38764544 | bytes 44332296 | tf_op jit(solution)/shard_map/broadcast_in_dim | solution.py:115
  660.8 10.4 %psum.51 = f32[]{:T(128)} all-reduce(f32[]{:T(128)} %subtract_reduce_fusion), channel_id=1, replica_groups=mesh['section'=4,'tensor'=8] {'section'}, use_global_device_ids=true, to_apply=%region_5.6 | all-reduce | flops 1 | bytes 8 | tf_op jit(solution)/shard_map/psum | solution.py:63
  (57 shorter events, 16.7 us)
Async XLA Ops:
  7.2 1.2 copy-start
  7.2 31.8 %all-gather.3.cloned.1.call-start = ((), (), s32[]{:S(2)}) async-start(), calls=%async_computation.1 | async-start | bytes 1916928 | tf_op jit(solution)/shard_map/all_gather | solution.py:32
  9.1 133.9 %reduce-scatter.4.cloned.1.call-start = ((), (), s32[]{:S(2)}) async-start(), calls=%async_computation.2 | async-start | bytes 3833856
  76.2 20.9 %copy-start.8 = (f32[128]{0:T(128)}, f32[128]{0:T(128)S(1)}, u32[]{:S(2)}) copy-start(f32[128]{0:T(128)S(1)} %psum.49) | copy-start | bytes 1540
  76.2 26.0 %copy-start.2 = (bf16[1,512,832]{1,2,0:T(8,128)(2,1)S(1)}, bf16[1,512,832]{1,2,0:T(8,128)(2,1)}, u32[]{:S(2)}) copy-start(bf16[1,512,832]{1,2,0:T(8,128)(2,1)} %param.12) | copy-start | bytes 2555908
  76.2 26.6 %copy-start.6 = (f32[1,832]{1,0:T(1,128)S(1)}, f32[1,832]{1,0:T(1,128)}, u32[]{:S(2)}) copy-start(f32[1,832]{1,0:T(1,128)} %param.14) | copy-start | bytes 9988
  76.2 27.2 %copy-start.4 = (f32[1,6656]{1,0:T(1,128)S(1)}, f32[1,6656]{1,0:T(1,128)}, u32[]{:S(2)}) copy-start(f32[1,6656]{1,0:T(1,128)} %param.15) | copy-start | bytes 79876
  157.3 71.2 %all-gather.5.cloned.1.call-start = ((), (), s32[]{:S(2)}) async-start(), calls=%async_computation.3 | async-start | bytes 7667712 | tf_op jit(solution)/shard_map/while/body/eval_jaxpr/all_gather | solution.py:67
  240.1 23.0 %collective-permute-start = (bf16[512,832]{0,1:T(8,128)(2,1)S(1)}, bf16[512,832]{0,1:T(8,128)(2,1)S(1)}, u32[]{:S(2)}, u32[]{:S(2)}) collective-permute-start(bf16[512,832]{0,1:T(8,128)(2,1)S(1)} %get-tuple-element.358), channel_id=1, source_target_pairs={{8,0},{16,8},{24,16},{9,1},{17,9},{25,17},{10,2},{18,10},{26,18},{... | collective-permute-start | bytes 2555912 | tf_op jit(solution)/shard_map/while/body/eval_jaxpr/ppermute | solution.py:14
  263.1 70.4 %all-gather.5.cloned.1.call-start = ((), (), s32[]{:S(2)}) async-start(), calls=%async_computation.3 | async-start | bytes 7667712 | tf_op jit(solution)/shard_map/while/body/eval_jaxpr/all_gather | solution.py:67
  345.2 23.0 %collective-permute-start = (bf16[512,832]{0,1:T(8,128)(2,1)S(1)}, bf16[512,832]{0,1:T(8,128)(2,1)S(1)}, u32[]{:S(2)}, u32[]{:S(2)}) collective-permute-start(bf16[512,832]{0,1:T(8,128)(2,1)S(1)} %get-tuple-element.358), channel_id=1, source_target_pairs={{8,0},{16,8},{24,16},{9,1},{17,9},{25,17},{10,2},{18,10},{26,18},{... | collective-permute-start | bytes 2555912 | tf_op jit(solution)/shard_map/while/body/eval_jaxpr/ppermute | solution.py:14
  368.2 70.4 %all-gather.5.cloned.1.call-start = ((), (), s32[]{:S(2)}) async-start(), calls=%async_computation.3 | async-start | bytes 7667712 | tf_op jit(solution)/shard_map/while/body/eval_jaxpr/all_gather | solution.py:67
  450.2 23.0 %collective-permute-start = (bf16[512,832]{0,1:T(8,128)(2,1)S(1)}, bf16[512,832]{0,1:T(8,128)(2,1)S(1)}, u32[]{:S(2)}, u32[]{:S(2)}) collective-permute-start(bf16[512,832]{0,1:T(8,128)(2,1)S(1)} %get-tuple-element.358), channel_id=1, source_target_pairs={{8,0},{16,8},{24,16},{9,1},{17,9},{25,17},{10,2},{18,10},{26,18},{... | collective-permute-start | bytes 2555912 | tf_op jit(solution)/shard_map/while/body/eval_jaxpr/ppermute | solution.py:14
  473.2 70.4 %all-gather.5.cloned.1.call-start = ((), (), s32[]{:S(2)}) async-start(), calls=%async_computation.3 | async-start | bytes 7667712 | tf_op jit(solution)/shard_map/while/body/eval_jaxpr/all_gather | solution.py:67
  555.3 23.0 %collective-permute-start = (bf16[512,832]{0,1:T(8,128)(2,1)S(1)}, bf16[512,832]{0,1:T(8,128)(2,1)S(1)}, u32[]{:S(2)}, u32[]{:S(2)}) collective-permute-start(bf16[512,832]{0,1:T(8,128)(2,1)S(1)} %get-tuple-element.358), channel_id=1, source_target_pairs={{8,0},{16,8},{24,16},{9,1},{17,9},{25,17},{10,2},{18,10},{26,18},{... | collective-permute-start | bytes 2555912 | tf_op jit(solution)/shard_map/while/body/eval_jaxpr/ppermute | solution.py:14
  578.2 9.7 %copy-start.5 = (f32[832]{0:T(1024)S(1)}, f32[832]{0:T(1024)}, u32[]{:S(2)}) copy-start(f32[832]{0:T(1024)} %multiply_reduce_fusion.2) | copy-start | bytes 9988
  578.2 36.4 %copy-start.3 = (f32[6656]{0:T(1024)S(1)}, f32[6656]{0:T(1024)}, u32[]{:S(2)}) copy-start(f32[6656]{0:T(1024)} %multiply_reduce_fusion.1) | copy-start | bytes 79876
  578.3 48.3 %copy-start.10 = (f32[128]{0:T(128)S(1)}, f32[128]{0:T(128)}, u32[]{:S(2)}) copy-start(f32[128]{0:T(128)} %get-tuple-element.271) | copy-start | bytes 1540
  642.1 30.4 %copy-start.1 = (bf16[512,832]{0,1:T(8,128)(2,1)S(1)}, bf16[512,832]{0,1:T(8,128)(2,1)}, u32[]{:S(2)}) copy-start(bf16[512,832]{0,1:T(8,128)(2,1)} %param.9) | copy-start | bytes 2555908
  642.2 17.4 %copy-start.9 = (f32[128]{0:T(128)S(1)}, f32[128]{0:T(128)}, u32[]{:S(2)}) copy-start(f32[128]{0:T(128)} %copy-done.8) | copy-start | bytes 1540
  642.2 29.1 %copy-start.7 = (f32[1,832]{1,0:T(1,128)S(1)}, f32[1,832]{1,0:T(1,128)}, u32[]{:S(2)}) copy-start(f32[1,832]{1,0:T(1,128)} %param.14) | copy-start | bytes 9988
Sparse Core Ops, SparseCore 0:
  10.2 28.7 all-gather.2
  102.3 40.6 reduce-scatter.3
  160.3 68.1 all-gather.4
  265.8 67.6 all-gather.4
  370.9 67.6 all-gather.4
  475.9 67.6 all-gather.4
where the time goes:
time: 681 us
  waiting for transfers between devices  360 us (53%)
  matrix products  152 us (22%)
  blocking collectives  78.4 us (12%)
  other arithmetic  56.9 us (8%)
  between operations  17.4 us (3%)
  local copies, waits for them, and re-layouts  10.6 us (2%)
    all_gather x4, waiting for transfers between devices, layer_block(): gathered = lax.all_gather(dy_rows, 'tensor', axis=1, tiled=True)  278 us
    dot_general x4, matrix products, layer_block(): lax.dot_general(saved_rows, gathered, (((0,), (0,)), ((), ())), preferred...  62.6 us
    dot_general x4, matrix products, layer_block(): lax.dot_general(gathered, local_weight, (((1,), (1,)), ((), ())), preferr...  46.7 us
    psum x2, blocking collectives, body(): lax.psum((jnp.sum(exponent, axis=1), jnp.sum(jnp.where(label_hit, logits,...  29.4 us
    all_gather x1, waiting for transfers between devices, body(): lax.all_gather(hidden_rows, 'tensor', axis=1, tiled=True)  29.1 us
    unnamed x3, waiting for transfers between devices  28.1 us
    psum x1, blocking collectives, body(): lax.psum((col_part, jnp.sum(row_new), jnp.sum(weight_float * weight_float...  26 us
    ppermute x4, waiting for transfers between devices, shifted(): return lax.ppermute(block, axis, route)  24.1 us
  transfers between devices with their start and end apart: 10, of which 10 were waited for; matrix products, arithmetic and copies ran while one was open for 11% of the time, Pallas kernels for 0%

commit v1 on v0

--- a/solution.py
+++ b/solution.py
@@ -64,7 +64,14 @@
     is_last = section_index == section_count - 1
 
     def layer_block(dy_rows, saved_rows):
-        gathered = lax.all_gather(dy_rows, "tensor", axis=1, tiled=True)
+        count = lax.axis_size("tensor")
+        forward = [(i_2, (i_2 + 1) % count) for i_2 in range(count)]
+        terms = [dy_rows]
+        for reach in range(1, count):
+            terms = [lax.ppermute(terms[0], "tensor", forward), *terms]
+        whole = jnp.concatenate(terms, axis=1)
+        turn = (lax.axis_index("tensor") + 1) * terms[-1].shape[1]
+        gathered = jnp.roll(whole, turn, axis=1)
         backward = lax.dot_general(
             gathered, local_weight, (((1,), (1,)), ((), ())), preferred_element_type=jnp.float32
         )

time: 681 us -> 828 us (1.22)
  waiting for transfers between devices: 360 us -> 448 us
  local copies, waits for them, and re-layouts: 10.6 us -> 51.9 us
    ppermute x0 -> x28, waiting for transfers between devices: none -> 391 us  [layer_block(): terms = [lax.ppermute(terms[0], 'tensor', forward), *terms]]
    all_gather x4 -> x0, waiting for transfers between devices: 278 us -> none  [layer_block(): gathered = lax.all_gather(dy_rows, 'tensor', axis=1, tiled=True)]
    while x0 -> x124, local copies, waits for them, and re-layouts: none -> 38.7 us
    ppermute x4, waiting for transfers between devices: 24.1 us -> 0.1 us  [shifted(): return lax.ppermute(block, axis, route)]
  transfers between devices with their start and end apart: 10 -> 34, of which waited for: 10 -> 31; matrix products, arithmetic and copies ran while one was open for 11% -> 10% of each run, Pallas kernels for 0% -> 0%
where the time goes in v1:
time: 828 us; the launch traced here: 826 us
  waiting for transfers between devices  448 us (54%)
  matrix products  160 us (19%)
  blocking collectives  84.8 us (10%)
  other arithmetic  57.9 us (7%)
  local copies, waits for them, and re-layouts  51.9 us (6%)
  between operations  17.4 us (2%)
    ppermute x28, waiting for transfers between devices, layer_block(): terms = [lax.ppermute(terms[0], 'tensor', forward), *terms]  391 us
    dot_general x4, matrix products, layer_block(): lax.dot_general(saved_rows, gathered, (((0,), (0,)), ((), ())), preferred...  64.4 us
    dot_general x4, matrix products, layer_block(): lax.dot_general(gathered, local_weight, (((1,), (1,)), ((), ())), preferr...  52.8 us
    while x124, local copies, waits for them, and re-layouts  38.7 us
    psum x2, blocking collectives, body(): lax.psum((jnp.sum(exponent, axis=1), jnp.sum(jnp.where(label_hit, logits,...  29.4 us
    all_gather x1, waiting for transfers between devices, body(): lax.all_gather(hidden_rows, 'tensor', axis=1, tiled=True)  29.1 us
    unnamed x3, waiting for transfers between devices  27.5 us
    psum x1, blocking collectives, body(): lax.psum((col_part, jnp.sum(row_new), jnp.sum(weight_float * weight_float...  26 us
  transfers between devices with their start and end apart: 34, of which 31 were waited for; matrix products, arithmetic and copies ran while one was open for 10% of the time, Pallas kernels for 0%

profile of v1, /device:TPU:0, one launch (start us, length us, event | category | flops | bytes accessed | tf_op | source)
XLA Modules:
  0.0 826.3 jit_solution(12617137264919196985)
XLA Ops:
  9.9 29.1 %all-gather.2.cloned.1.call-done = bf16[128,6656]{0,1:T(8,128)(2,1)} async-done(((bf16[128,832]{0,1:T(8,128)(2,1)}), bf16[128,6656]{0,1:T(8,128)(2,1)}) %all-gather.2.cloned.1.call-update) | async-done | bytes 1703952 | tf_op jit(solution)/shard_map/all_gather | solution.py:32
  39.0 22.1 %exponential_reduce_fusion = (f32[128]{0:T(128)S(1)}, f32[128]{0:T(128)}, f32[128,4000]{0,1:T(8,128)S(1)}) fusion(s32[4000]{0:T(1024)S(1)} %iota_add_fusion, s32[128]{0:T(128)S(1)} %dynamic_slice.18, bf16[6656,4000]{0,1:T(8,128)(2,1)} %param.11, bf16[128,6656]{0,1:T(8,128)(2,1)} %all-gather.2.cloned.1.call-done), kind=kOutput, calls=%fused_computation.42 | convolution fusion | flops 6817792000 | bytes 57017472 | tf_op jit(solution)/shard_map/dot_general | solution.py:31
  61.0 15.1 %psum.49 = f32[128]{0:T(128)S(1)} all-reduce(f32[128]{0:T(128)S(1)} %get-tuple-element.282), channel_id=1, replica_groups=mesh['section'=4,'tensor'=8] {'tensor'}, use_global_device_ids=true, to_apply=%region_1.2 | all-reduce | flops 128 | bytes 1024 | tf_op jit(solution)/shard_map/psum | solution.py:40
  76.2 20.9 %convolution_bitcast_fusion = f32[6656,128]{0,1:T(8,128)} fusion(bf16[6656,4000]{0,1:T(8,128)(2,1)} %param.11, f32[128,4000]{0,1:T(8,128)S(1)} %get-tuple-element.312, f32[128]{0:T(128)S(1)} %psum.49, s32[128]{0:T(128)S(1)} %dynamic_slice.18, s32[4000]{0:T(1024)S(1)} %iota_add_fusion), kind=kOutput, calls=%fused_computation.35 | convolution fusion | flops 6818816000 | bytes 58720896 | tf_op jit(solution)/shard_map/dot_general | solution.py:53
  115.5 27.4 %reduce-scatter.4.cloned.1.call-done = f32[832,128]{1,0:T(8,128)} async-done(((f32[6656,128]{1,0:T(8,128)}), f32[832,128]{1,0:T(8,128)}) %reduce-scatter.4.cloned.1.call-update) | async-done | bytes 426000
  159.0 558.7 %while.20 = (s32[]{:T(128)}, bf16[512,832]{0,1:T(8,128)(2,1)}, f32[832,6656]{1,0:T(8,128)}, bf16[512,832]{0,1:T(8,128)(2,1)}, pred[]{:T(512)}, /*index=5*/bf16[5...) while((s32[]{:T(128)}, bf16[512,832]{0,1:T(8,128)(2,1)}, ...), condition=%wide.region_8.9_spmd.clone, body=%wide.region_7.8_spmd.clone.sunk | while | flops 11360567296 | bytes 208733072 | solution.py:102
  174.2 13.9 %collective-permute-done.1 = bf16[512,832]{0,1:T(8,128)(2,1)S(1)} collective-permute-done((bf16[512,832]{0,1:T(8,128)(2,1)S(1)}, bf16[512,832]{0,1:T(8,128)(2,1)S(1)}, u32[]{:S(2)}, u32[]{:S(2)}) %collective-permute-start.1) | collective-permute-done | bytes 852000 | tf_op jit(solution)/shard_map/while/body/eval_jaxpr/ppermute | solution.py:71
  188.1 13.9 %collective-permute-done.2 = bf16[512,832]{0,1:T(8,128)(2,1)S(1)} collective-permute-done((bf16[512,832]{0,1:T(8,128)(2,1)S(1)}, bf16[512,832]{0,1:T(8,128)(2,1)S(1)}, u32[]{:S(2)}, u32[]{:S(2)}) %collective-permute-start.2) | collective-permute-done | bytes 852000 | tf_op jit(solution)/shard_map/while/body/eval_jaxpr/ppermute | solution.py:71
  202.1 13.9 %collective-permute-done.3 = bf16[512,832]{0,1:T(8,128)(2,1)S(1)} collective-permute-done((bf16[512,832]{0,1:T(8,128)(2,1)S(1)}, bf16[512,832]{0,1:T(8,128)(2,1)S(1)}, u32[]{:S(2)}, u32[]{:S(2)}) %collective-permute-start.3) | collective-permute-done | bytes 852000 | tf_op jit(solution)/shard_map/while/body/eval_jaxpr/ppermute | solution.py:71
  216.9 13.9 %collective-permute-done.4 = bf16[512,832]{0,1:T(8,128)(2,1)S(1)} collective-permute-done((bf16[512,832]{0,1:T(8,128)(2,1)S(1)}, bf16[512,832]{0,1:T(8,128)(2,1)S(1)}, u32[]{:S(2)}, u32[]{:S(2)}) %collective-permute-start.4) | collective-permute-done | bytes 852000 | tf_op jit(solution)/shard_map/while/body/eval_jaxpr/ppermute | solution.py:71
  231.7 14.0 %collective-permute-done.5 = bf16[512,832]{0,1:T(8,128)(2,1)} collective-permute-done((bf16[512,832]{0,1:T(8,128)(2,1)S(1)}, bf16[512,832]{0,1:T(8,128)(2,1)}, u32[]{:S(2)}, u32[]{:S(2)}) %collective-permute-start.5) | collective-permute-done | bytes 852000 | tf_op jit(solution)/shard_map/while/body/eval_jaxpr/ppermute | solution.py:71
  245.8 14.2 %collective-permute-done.6 = bf16[512,832]{0,1:T(8,128)(2,1)} collective-permute-done((bf16[512,832]{0,1:T(8,128)(2,1)}, bf16[512,832]{0,1:T(8,128)(2,1)}, u32[]{:S(2)}, u32[]{:S(2)}) %collective-permute-start.6) | collective-permute-done | bytes 852000 | tf_op jit(solution)/shard_map/while/body/eval_jaxpr/ppermute | solution.py:71
  311.1 13.9 %collective-permute-done.1 = bf16[512,832]{0,1:T(8,128)(2,1)S(1)} collective-permute-done((bf16[512,832]{0,1:T(8,128)(2,1)S(1)}, bf16[512,832]{0,1:T(8,128)(2,1)S(1)}, u32[]{:S(2)}, u32[]{:S(2)}) %collective-permute-start.1) | collective-permute-done | bytes 852000 | tf_op jit(solution)/shard_map/while/body/eval_jaxpr/ppermute | solution.py:71
  325.0 13.9 %collective-permute-done.2 = bf16[512,832]{0,1:T(8,128)(2,1)S(1)} collective-permute-done((bf16[512,832]{0,1:T(8,128)(2,1)S(1)}, bf16[512,832]{0,1:T(8,128)(2,1)S(1)}, u32[]{:S(2)}, u32[]{:S(2)}) %collective-permute-start.2) | collective-permute-done | bytes 852000 | tf_op jit(solution)/shard_map/while/body/eval_jaxpr/ppermute | solution.py:71
  339.0 13.9 %collective-permute-done.3 = bf16[512,832]{0,1:T(8,128)(2,1)S(1)} collective-permute-done((bf16[512,832]{0,1:T(8,128)(2,1)S(1)}, bf16[512,832]{0,1:T(8,128)(2,1)S(1)}, u32[]{:S(2)}, u32[]{:S(2)}) %collective-permute-start.3) | collective-permute-done | bytes 852000 | tf_op jit(solution)/shard_map/while/body/eval_jaxpr/ppermute | solution.py:71
  353.8 13.9 %collective-permute-done.4 = bf16[512,832]{0,1:T(8,128)(2,1)S(1)} collective-permute-done((bf16[512,832]{0,1:T(8,128)(2,1)S(1)}, bf16[512,832]{0,1:T(8,128)(2,1)S(1)}, u32[]{:S(2)}, u32[]{:S(2)}) %collective-permute-start.4) | collective-permute-done | bytes 852000 | tf_op jit(solution)/shard_map/while/body/eval_jaxpr/ppermute | solution.py:71
  368.6 14.0 %collective-permute-done.5 = bf16[512,832]{0,1:T(8,128)(2,1)} collective-permute-done((bf16[512,832]{0,1:T(8,128)(2,1)S(1)}, bf16[512,832]{0,1:T(8,128)(2,1)}, u32[]{:S(2)}, u32[]{:S(2)}) %collective-permute-start.5) | collective-permute-done | bytes 852000 | tf_op jit(solution)/shard_map/while/body/eval_jaxpr/ppermute | solution.py:71
  382.7 14.2 %collective-permute-done.6 = bf16[512,832]{0,1:T(8,128)(2,1)} collective-permute-done((bf16[512,832]{0,1:T(8,128)(2,1)}, bf16[512,832]{0,1:T(8,128)(2,1)}, u32[]{:S(2)}, u32[]{:S(2)}) %collective-permute-start.6) | collective-permute-done | bytes 852000 | tf_op jit(solution)/shard_map/while/body/eval_jaxpr/ppermute | solution.py:71
  419.5 17.0 %bitcast_add_fusion.2 = f32[832,6656]{1,0:T(8,128)} fusion(f32[832,6656]{1,0:T(8,128)} %get-tuple-element.389, bf16[512,832]{1,0:T(8,128)(2,1)S(1)} %copy-done.7, pred[]{:T(512)S(6)} %compare.3, pred[]{:T(512)S(6)} %eq.62, bf16[512,13312]{0,1:T(8,128)(2,1)} %copy-done.2, s32[]{:T(128)S(6)} %select_n.143), kind=kOutput, calls=%fused_computation.clone.1 | convolution fusion | flops 5687312384 | bytes 51970056 | tf_op jit(solution)/shard_map/while/body/eval_jaxpr/dot_general | solution.py:78
  451.7 13.9 %collective-permute-done.1 = bf16[512,832]{0,1:T(8,128)(2,1)S(1)} collective-permute-done((bf16[512,832]{0,1:T(8,128)(2,1)S(1)}, bf16[512,832]{0,1:T(8,128)(2,1)S(1)}, u32[]{:S(2)}, u32[]{:S(2)}) %collective-permute-start.1) | collective-permute-done | bytes 852000 | tf_op jit(solution)/shard_map/while/body/eval_jaxpr/ppermute | solution.py:71
  465.6 13.9 %collective-permute-done.2 = bf16[512,832]{0,1:T(8,128)(2,1)S(1)} collective-permute-done((bf16[512,832]{0,1:T(8,128)(2,1)S(1)}, bf16[512,832]{0,1:T(8,128)(2,1)S(1)}, u32[]{:S(2)}, u32[]{:S(2)}) %collective-permute-start.2) | collective-permute-done | bytes 852000 | tf_op jit(solution)/shard_map/while/body/eval_jaxpr/ppermute | solution.py:71
  479.6 13.9 %collective-permute-done.3 = bf16[512,832]{0,1:T(8,128)(2,1)S(1)} collective-permute-done((bf16[512,832]{0,1:T(8,128)(2,1)S(1)}, bf16[512,832]{0,1:T(8,128)(2,1)S(1)}, u32[]{:S(2)}, u32[]{:S(2)}) %collective-permute-start.3) | collective-permute-done | bytes 852000 | tf_op jit(solution)/shard_map/while/body/eval_jaxpr/ppermute | solution.py:71
  509.2 14.0 %collective-permute-done.5 = bf16[512,832]{0,1:T(8,128)(2,1)} collective-permute-done((bf16[512,832]{0,1:T(8,128)(2,1)S(1)}, bf16[512,832]{0,1:T(8,128)(2,1)}, u32[]{:S(2)}, u32[]{:S(2)}) %collective-permute-start.5) | collective-permute-done | bytes 852000 | tf_op jit(solution)/shard_map/while/body/eval_jaxpr/ppermute | solution.py:71
  523.3 14.2 %collective-permute-done.6 = bf16[512,832]{0,1:T(8,128)(2,1)} collective-permute-done((bf16[512,832]{0,1:T(8,128)(2,1)}, bf16[512,832]{0,1:T(8,128)(2,1)}, u32[]{:S(2)}, u32[]{:S(2)}) %collective-permute-start.6) | collective-permute-done | bytes 852000 | tf_op jit(solution)/shard_map/while/body/eval_jaxpr/ppermute | solution.py:71
  560.0 17.0 %bitcast_add_fusion.2 = f32[832,6656]{1,0:T(8,128)} fusion(f32[832,6656]{1,0:T(8,128)} %get-tuple-element.389, bf16[512,832]{1,0:T(8,128)(2,1)S(1)} %copy-done.7, pred[]{:T(512)S(6)} %compare.3, pred[]{:T(512)S(6)} %eq.62, bf16[512,13312]{0,1:T(8,128)(2,1)} %copy-done.2, s32[]{:T(128)S(6)} %select_n.143), kind=kOutput, calls=%fused_computation.clone.1 | convolution fusion | flops 5687312384 | bytes 51970056 | tf_op jit(solution)/shard_map/while/body/eval_jaxpr/dot_general | solution.py:78
  649.8 14.0 %collective-permute-done.5 = bf16[512,832]{0,1:T(8,128)(2,1)} collective-permute-done((bf16[512,832]{0,1:T(8,128)(2,1)S(1)}, bf16[512,832]{0,1:T(8,128)(2,1)}, u32[]{:S(2)}, u32[]{:S(2)}) %collective-permute-start.5) | collective-permute-done | bytes 852000 | tf_op jit(solution)/shard_map/while/body/eval_jaxpr/ppermute | solution.py:71
  663.9 14.2 %collective-permute-done.6 = bf16[512,832]{0,1:T(8,128)(2,1)} collective-permute-done((bf16[512,832]{0,1:T(8,128)(2,1)}, bf16[512,832]{0,1:T(8,128)(2,1)}, u32[]{:S(2)}, u32[]{:S(2)}) %collective-permute-start.6) | collective-permute-done | bytes 852000 | tf_op jit(solution)/shard_map/while/body/eval_jaxpr/ppermute | solution.py:71
  700.6 17.0 %bitcast_add_fusion.2 = f32[832,6656]{1,0:T(8,128)} fusion(f32[832,6656]{1,0:T(8,128)} %get-tuple-element.389, bf16[512,832]{1,0:T(8,128)(2,1)S(1)} %copy-done.7, pred[]{:T(512)S(6)} %compare.3, pred[]{:T(512)S(6)} %eq.62, bf16[512,13312]{0,1:T(8,128)(2,1)} %copy-done.2, s32[]{:T(128)S(6)} %select_n.143), kind=kOutput, calls=%fused_computation.clone.1 | convolution fusion | flops 5687312384 | bytes 51970056 | tf_op jit(solution)/shard_map/while/body/eval_jaxpr/dot_general | solution.py:78
  728.0 26.0 %all-reduce.1 = (f32[]{:T(128)}, f32[6656]{0:T(1024)S(1)}) all-reduce(f32[]{:T(128)} %get-tuple-element.307, f32[6656]{0:T(1024)S(1)} %get-tuple-element.280), channel_id=1, replica_groups=mesh['section'=4,'tensor'=8] {'tensor'}, use_global_device_ids=true, to_apply=%region_15.16 | all-reduce | flops 6657 | bytes 53256 | tf_op jit(solution)/shard_map/psum | solution.py:110
  766.0 14.2 %all-reduce = (f32[128]{0:T(128)S(1)}, f32[]{:T(128)}, f32[]{:T(128)}) all-reduce(f32[128]{0:T(128)S(1)} %copy-done.18, f32[]{:T(128)} %fusion.7, f32[]{:T(128)} %multiply_reduce_fusion), channel_id=1, replica_groups=mesh['section'=4,'tensor'=8] {'tensor'}, use_global_device_ids=true, to_apply=%region_3.4 | all-reduce | flops 130 | bytes 1040 | tf_op jit(solution)/shard_map/psum | solution.py:40
  781.7 17.4 %fusion.11 = bf16[1,832,6656]{2,1,0:T(8,128)(2,1)} fusion(f32[]{:T(128)S(6)} %div.49, bf16[1,832,6656]{2,1,0:T(8,128)(2,1)} %bitcast.27, f32[832,6656]{1,0:T(8,128)} %get-tuple-element.231, f32[]{:T(128)} %get-tuple-element.305, f32[6656]{0:T(1024)S(1)} %multiply_add_fusion.1, f32[832]{0:T(1024)S(1)} %get-tuple-element.308), kind=kLoop, calls=%fused_computation.34 | loop fusion | flops 38764544 | bytes 44332296 | tf_op jit(solution)/shard_map/broadcast_in_dim | solution.py:122
  800.3 16.8 %psum.51 = f32[]{:T(128)} all-reduce(f32[]{:T(128)} %subtract_reduce_fusion), channel_id=1, replica_groups=mesh['section'=4,'tensor'=8] {'section'}, use_global_device_ids=true, to_apply=%region_5.6 | all-reduce | flops 1 | bytes 8 | tf_op jit(solution)/shard_map/psum | solution.py:63
  (229 shorter events, 302.0 us)
Async XLA Ops:
  7.2 31.8 %all-gather.2.cloned.1.call-start = ((), (), s32[]{:S(2)}) async-start(), calls=%async_computation.1 | async-start | bytes 1916928 | tf_op jit(solution)/shard_map/all_gather | solution.py:32
  9.1 133.9 %reduce-scatter.4.cloned.1.call-start = ((), (), s32[]{:S(2)}) async-start(), calls=%async_computation.2 | async-start | bytes 3833856
  160.3 14.0 %collective-permute-start = (bf16[512,832]{0,1:T(8,128)(2,1)S(1)}, bf16[512,832]{0,1:T(8,128)(2,1)S(1)}, u32[]{:S(2)}, u32[]{:S(2)}) collective-permute-start(bf16[512,832]{0,1:T(8,128)(2,1)S(1)} %broadcast_select_fusion.2), channel_id=1, source_target_pairs={{0,1},{1,2},{2,3},{3,4},{4,5},{5,6},{6,7},{7,0},{8,9},{9,10},{10,1... | collective-permute-start | bytes 2555912 | tf_op jit(solution)/shard_map/while/body/eval_jaxpr/ppermute | solution.py:71
  174.2 13.9 %collective-permute-start.1 = (bf16[512,832]{0,1:T(8,128)(2,1)S(1)}, bf16[512,832]{0,1:T(8,128)(2,1)S(1)}, u32[]{:S(2)}, u32[]{:S(2)}) collective-permute-start(bf16[512,832]{0,1:T(8,128)(2,1)S(1)} %collective-permute-done), channel_id=1, source_target_pairs={{0,1},{1,2},{2,3},{3,4},{4,5},{5,6},{6,7},{7,0},{8,9},{9,10},{10,1... | collective-permute-start | bytes 2555912 | tf_op jit(solution)/shard_map/while/body/eval_jaxpr/ppermute | solution.py:71
  188.1 13.9 %collective-permute-start.2 = (bf16[512,832]{0,1:T(8,128)(2,1)S(1)}, bf16[512,832]{0,1:T(8,128)(2,1)S(1)}, u32[]{:S(2)}, u32[]{:S(2)}) collective-permute-start(bf16[512,832]{0,1:T(8,128)(2,1)S(1)} %collective-permute-done.1), channel_id=1, source_target_pairs={{0,1},{1,2},{2,3},{3,4},{4,5},{5,6},{6,7},{7,0},{8,9},{9,10},{10,1... | collective-permute-start | bytes 2555912 | tf_op jit(solution)/shard_map/while/body/eval_jaxpr/ppermute | solution.py:71
  202.1 13.9 %collective-permute-start.3 = (bf16[512,832]{0,1:T(8,128)(2,1)S(1)}, bf16[512,832]{0,1:T(8,128)(2,1)S(1)}, u32[]{:S(2)}, u32[]{:S(2)}) collective-permute-start(bf16[512,832]{0,1:T(8,128)(2,1)S(1)} %collective-permute-done.2), channel_id=1, source_target_pairs={{0,1},{1,2},{2,3},{3,4},{4,5},{5,6},{6,7},{7,0},{8,9},{9,10},{10,1... | collective-permute-start | bytes 2555912 | tf_op jit(solution)/shard_map/while/body/eval_jaxpr/ppermute | solution.py:71
  216.9 13.9 %collective-permute-start.4 = (bf16[512,832]{0,1:T(8,128)(2,1)S(1)}, bf16[512,832]{0,1:T(8,128)(2,1)S(1)}, u32[]{:S(2)}, u32[]{:S(2)}) collective-permute-start(bf16[512,832]{0,1:T(8,128)(2,1)S(1)} %collective-permute-done.3), channel_id=1, source_target_pairs={{0,1},{1,2},{2,3},{3,4},{4,5},{5,6},{6,7},{7,0},{8,9},{9,10},{10,1... | collective-permute-start | bytes 2555912 | tf_op jit(solution)/shard_map/while/body/eval_jaxpr/ppermute | solution.py:71
  231.7 14.0 %collective-permute-start.5 = (bf16[512,832]{0,1:T(8,128)(2,1)S(1)}, bf16[512,832]{0,1:T(8,128)(2,1)}, u32[]{:S(2)}, u32[]{:S(2)}) collective-permute-start(bf16[512,832]{0,1:T(8,128)(2,1)S(1)} %collective-permute-done.4), channel_id=1, source_target_pairs={{0,1},{1,2},{2,3},{3,4},{4,5},{5,6},{6,7},{7,0},{8,9},{9,10},{10,1... | collective-permute-start | bytes 2555912 | tf_op jit(solution)/shard_map/while/body/eval_jaxpr/ppermute | solution.py:71
  245.8 14.2 %collective-permute-start.6 = (bf16[512,832]{0,1:T(8,128)(2,1)}, bf16[512,832]{0,1:T(8,128)(2,1)}, u32[]{:S(2)}, u32[]{:S(2)}) collective-permute-start(bf16[512,832]{0,1:T(8,128)(2,1)} %collective-permute-done.5), channel_id=1, source_target_pairs={{0,1},{1,2},{2,3},{3,4},{4,5},{5,6},{6,7},{7,0},{8,9},{9,10},{10,1... | collective-permute-start | bytes 2555912 | tf_op jit(solution)/shard_map/while/body/eval_jaxpr/ppermute | solution.py:71
  281.2 14.7 %collective-permute-start.7 = (bf16[512,832]{0,1:T(8,128)(2,1)S(1)}, bf16[512,832]{0,1:T(8,128)(2,1)}, u32[]{:S(2)}, u32[]{:S(2)}) collective-permute-start(bf16[512,832]{0,1:T(8,128)(2,1)S(1)} %get-tuple-element.370), channel_id=1, source_target_pairs={{8,0},{16,8},{24,16},{9,1},{17,9},{25,17},{10,2},{18,10},{26,18},{... | collective-permute-start | bytes 2555912 | tf_op jit(solution)/shard_map/while/body/eval_jaxpr/ppermute | solution.py:14
  297.2 14.0 %collective-permute-start = (bf16[512,832]{0,1:T(8,128)(2,1)S(1)}, bf16[512,832]{0,1:T(8,128)(2,1)S(1)}, u32[]{:S(2)}, u32[]{:S(2)}) collective-permute-start(bf16[512,832]{0,1:T(8,128)(2,1)S(1)} %broadcast_select_fusion.2), channel_id=1, source_target_pairs={{0,1},{1,2},{2,3},{3,4},{4,5},{5,6},{6,7},{7,0},{8,9},{9,10},{10,1... | collective-permute-start | bytes 2555912 | tf_op jit(solution)/shard_map/while/body/eval_jaxpr/ppermute | solution.py:71
  311.1 13.9 %collective-permute-start.1 = (bf16[512,832]{0,1:T(8,128)(2,1)S(1)}, bf16[512,832]{0,1:T(8,128)(2,1)S(1)}, u32[]{:S(2)}, u32[]{:S(2)}) collective-permute-start(bf16[512,832]{0,1:T(8,128)(2,1)S(1)} %collective-permute-done), channel_id=1, source_target_pairs={{0,1},{1,2},{2,3},{3,4},{4,5},{5,6},{6,7},{7,0},{8,9},{9,10},{10,1... | collective-permute-start | bytes 2555912 | tf_op jit(solution)/shard_map/while/body/eval_jaxpr/ppermute | solution.py:71
  325.0 13.9 %collective-permute-start.2 = (bf16[512,832]{0,1:T(8,128)(2,1)S(1)}, bf16[512,832]{0,1:T(8,128)(2,1)S(1)}, u32[]{:S(2)}, u32[]{:S(2)}) collective-permute-start(bf16[512,832]{0,1:T(8,128)(2,1)S(1)} %collective-permute-done.1), channel_id=1, source_target_pairs={{0,1},{1,2},{2,3},{3,4},{4,5},{5,6},{6,7},{7,0},{8,9},{9,10},{10,1... | collective-permute-start | bytes 2555912 | tf_op jit(solution)/shard_map/while/body/eval_jaxpr/ppermute | solution.py:71
  339.0 13.9 %collective-permute-start.3 = (bf16[512,832]{0,1:T(8,128)(2,1)S(1)}, bf16[512,832]{0,1:T(8,128)(2,1)S(1)}, u32[]{:S(2)}, u32[]{:S(2)}) collective-permute-start(bf16[512,832]{0,1:T(8,128)(2,1)S(1)} %collective-permute-done.2), channel_id=1, source_target_pairs={{0,1},{1,2},{2,3},{3,4},{4,5},{5,6},{6,7},{7,0},{8,9},{9,10},{10,1... | collective-permute-start | bytes 2555912 | tf_op jit(solution)/shard_map/while/body/eval_jaxpr/ppermute | solution.py:71
  353.8 13.9 %collective-permute-start.4 = (bf16[512,832]{0,1:T(8,128)(2,1)S(1)}, bf16[512,832]{0,1:T(8,128)(2,1)S(1)}, u32[]{:S(2)}, u32[]{:S(2)}) collective-permute-start(bf16[512,832]{0,1:T(8,128)(2,1)S(1)} %collective-permute-done.3), channel_id=1, source_target_pairs={{0,1},{1,2},{2,3},{3,4},{4,5},{5,6},{6,7},{7,0},{8,9},{9,10},{10,1... | collective-permute-start | bytes 2555912 | tf_op jit(solution)/shard_map/while/body/eval_jaxpr/ppermute | solution.py:71
  368.6 14.0 %collective-permute-start.5 = (bf16[512,832]{0,1:T(8,128)(2,1)S(1)}, bf16[512,832]{0,1:T(8,128)(2,1)}, u32[]{:S(2)}, u32[]{:S(2)}) collective-permute-start(bf16[512,832]{0,1:T(8,128)(2,1)S(1)} %collective-permute-done.4), channel_id=1, source_target_pairs={{0,1},{1,2},{2,3},{3,4},{4,5},{5,6},{6,7},{7,0},{8,9},{9,10},{10,1... | collective-permute-start | bytes 2555912 | tf_op jit(solution)/shard_map/while/body/eval_jaxpr/ppermute | solution.py:71
  382.7 14.2 %collective-permute-start.6 = (bf16[512,832]{0,1:T(8,128)(2,1)}, bf16[512,832]{0,1:T(8,128)(2,1)}, u32[]{:S(2)}, u32[]{:S(2)}) collective-permute-start(bf16[512,832]{0,1:T(8,128)(2,1)} %collective-permute-done.5), channel_id=1, source_target_pairs={{0,1},{1,2},{2,3},{3,4},{4,5},{5,6},{6,7},{7,0},{8,9},{9,10},{10,1... | collective-permute-start | bytes 2555912 | tf_op jit(solution)/shard_map/while/body/eval_jaxpr/ppermute | solution.py:71
  418.1 18.4 %collective-permute-start.7 = (bf16[512,832]{0,1:T(8,128)(2,1)S(1)}, bf16[512,832]{0,1:T(8,128)(2,1)}, u32[]{:S(2)}, u32[]{:S(2)}) collective-permute-start(bf16[512,832]{0,1:T(8,128)(2,1)S(1)} %get-tuple-element.370), channel_id=1, source_target_pairs={{8,0},{16,8},{24,16},{9,1},{17,9},{25,17},{10,2},{18,10},{26,18},{... | collective-permute-start | bytes 2555912 | tf_op jit(solution)/shard_map/while/body/eval_jaxpr/ppermute | solution.py:14
  437.8 14.0 %collective-permute-start = (bf16[512,832]{0,1:T(8,128)(2,1)S(1)}, bf16[512,832]{0,1:T(8,128)(2,1)S(1)}, u32[]{:S(2)}, u32[]{:S(2)}) collective-permute-start(bf16[512,832]{0,1:T(8,128)(2,1)S(1)} %broadcast_select_fusion.2), channel_id=1, source_target_pairs={{0,1},{1,2},{2,3},{3,4},{4,5},{5,6},{6,7},{7,0},{8,9},{9,10},{10,1... | collective-permute-start | bytes 2555912 | tf_op jit(solution)/shard_map/while/body/eval_jaxpr/ppermute | solution.py:71
  451.7 13.9 %collective-permute-start.1 = (bf16[512,832]{0,1:T(8,128)(2,1)S(1)}, bf16[512,832]{0,1:T(8,128)(2,1)S(1)}, u32[]{:S(2)}, u32[]{:S(2)}) collective-permute-start(bf16[512,832]{0,1:T(8,128)(2,1)S(1)} %collective-permute-done), channel_id=1, source_target_pairs={{0,1},{1,2},{2,3},{3,4},{4,5},{5,6},{6,7},{7,0},{8,9},{9,10},{10,1... | collective-permute-start | bytes 2555912 | tf_op jit(solution)/shard_map/while/body/eval_jaxpr/ppermute | solution.py:71
  465.6 13.9 %collective-permute-start.2 = (bf16[512,832]{0,1:T(8,128)(2,1)S(1)}, bf16[512,832]{0,1:T(8,128)(2,1)S(1)}, u32[]{:S(2)}, u32[]{:S(2)}) collective-permute-start(bf16[512,832]{0,1:T(8,128)(2,1)S(1)} %collective-permute-done.1), channel_id=1, source_target_pairs={{0,1},{1,2},{2,3},{3,4},{4,5},{5,6},{6,7},{7,0},{8,9},{9,10},{10,1... | collective-permute-start | bytes 2555912 | tf_op jit(solution)/shard_map/while/body/eval_jaxpr/ppermute | solution.py:71
  479.6 13.9 %collective-permute-start.3 = (bf16[512,832]{0,1:T(8,128)(2,1)S(1)}, bf16[512,832]{0,1:T(8,128)(2,1)S(1)}, u32[]{:S(2)}, u32[]{:S(2)}) collective-permute-start(bf16[512,832]{0,1:T(8,128)(2,1)S(1)} %collective-permute-done.2), channel_id=1, source_target_pairs={{0,1},{1,2},{2,3},{3,4},{4,5},{5,6},{6,7},{7,0},{8,9},{9,10},{10,1... | collective-permute-start | bytes 2555912 | tf_op jit(solution)/shard_map/while/body/eval_jaxpr/ppermute | solution.py:71
  494.4 13.9 %collective-permute-start.4 = (bf16[512,832]{0,1:T(8,128)(2,1)S(1)}, bf16[512,832]{0,1:T(8,128)(2,1)S(1)}, u32[]{:S(2)}, u32[]{:S(2)}) collective-permute-start(bf16[512,832]{0,1:T(8,128)(2,1)S(1)} %collective-permute-done.3), channel_id=1, source_target_pairs={{0,1},{1,2},{2,3},{3,4},{4,5},{5,6},{6,7},{7,0},{8,9},{9,10},{10,1... | collective-permute-start | bytes 2555912 | tf_op jit(solution)/shard_map/while/body/eval_jaxpr/ppermute | solution.py:71
  509.2 14.0 %collective-permute-start.5 = (bf16[512,832]{0,1:T(8,128)(2,1)S(1)}, bf16[512,832]{0,1:T(8,128)(2,1)}, u32[]{:S(2)}, u32[]{:S(2)}) collective-permute-start(bf16[512,832]{0,1:T(8,128)(2,1)S(1)} %collective-permute-done.4), channel_id=1, source_target_pairs={{0,1},{1,2},{2,3},{3,4},{4,5},{5,6},{6,7},{7,0},{8,9},{9,10},{10,1... | collective-permute-start | bytes 2555912 | tf_op jit(solution)/shard_map/while/body/eval_jaxpr/ppermute | solution.py:71
  523.3 14.2 %collective-permute-start.6 = (bf16[512,832]{0,1:T(8,128)(2,1)}, bf16[512,832]{0,1:T(8,128)(2,1)}, u32[]{:S(2)}, u32[]{:S(2)}) collective-permute-start(bf16[512,832]{0,1:T(8,128)(2,1)} %collective-permute-done.5), channel_id=1, source_target_pairs={{0,1},{1,2},{2,3},{3,4},{4,5},{5,6},{6,7},{7,0},{8,9},{9,10},{10,1... | collective-permute-start | bytes 2555912 | tf_op jit(solution)/shard_map/while/body/eval_jaxpr/ppermute | solution.py:71
  558.7 18.4 %collective-permute-start.7 = (bf16[512,832]{0,1:T(8,128)(2,1)S(1)}, bf16[512,832]{0,1:T(8,128)(2,1)}, u32[]{:S(2)}, u32[]{:S(2)}) collective-permute-start(bf16[512,832]{0,1:T(8,128)(2,1)S(1)} %get-tuple-element.370), channel_id=1, source_target_pairs={{8,0},{16,8},{24,16},{9,1},{17,9},{25,17},{10,2},{18,10},{26,18},{... | collective-permute-start | bytes 2555912 | tf_op jit(solution)/shard_map/while/body/eval_jaxpr/ppermute | solution.py:14
  578.3 14.0 %collective-permute-start = (bf16[512,832]{0,1:T(8,128)(2,1)S(1)}, bf16[512,832]{0,1:T(8,128)(2,1)S(1)}, u32[]{:S(2)}, u32[]{:S(2)}) collective-permute-start(bf16[512,832]{0,1:T(8,128)(2,1)S(1)} %broadcast_select_fusion.2), channel_id=1, source_target_pairs={{0,1},{1,2},{2,3},{3,4},{4,5},{5,6},{6,7},{7,0},{8,9},{9,10},{10,1... | collective-permute-start | bytes 2555912 | tf_op jit(solution)/shard_map/while/body/eval_jaxpr/ppermute | solution.py:71
  592.3 13.9 %collective-permute-start.1 = (bf16[512,832]{0,1:T(8,128)(2,1)S(1)}, bf16[512,832]{0,1:T(8,128)(2,1)S(1)}, u32[]{:S(2)}, u32[]{:S(2)}) collective-permute-start(bf16[512,832]{0,1:T(8,128)(2,1)S(1)} %collective-permute-done), channel_id=1, source_target_pairs={{0,1},{1,2},{2,3},{3,4},{4,5},{5,6},{6,7},{7,0},{8,9},{9,10},{10,1... | collective-permute-start | bytes 2555912 | tf_op jit(solution)/shard_map/while/body/eval_jaxpr/ppermute | solution.py:71
  606.2 13.9 %collective-permute-start.2 = (bf16[512,832]{0,1:T(8,128)(2,1)S(1)}, bf16[512,832]{0,1:T(8,128)(2,1)S(1)}, u32[]{:S(2)}, u32[]{:S(2)}) collective-permute-start(bf16[512,832]{0,1:T(8,128)(2,1)S(1)} %collective-permute-done.1), channel_id=1, source_target_pairs={{0,1},{1,2},{2,3},{3,4},{4,5},{5,6},{6,7},{7,0},{8,9},{9,10},{10,1... | collective-permute-start | bytes 2555912 | tf_op jit(solution)/shard_map/while/body/eval_jaxpr/ppermute | solution.py:71
  649.8 14.0 %collective-permute-start.5 = (bf16[512,832]{0,1:T(8,128)(2,1)S(1)}, bf16[512,832]{0,1:T(8,128)(2,1)}, u32[]{:S(2)}, u32[]{:S(2)}) collective-permute-start(bf16[512,832]{0,1:T(8,128)(2,1)S(1)} %collective-permute-done.4), channel_id=1, source_target_pairs={{0,1},{1,2},{2,3},{3,4},{4,5},{5,6},{6,7},{7,0},{8,9},{9,10},{10,1... | collective-permute-start | bytes 2555912 | tf_op jit(solution)/shard_map/while/body/eval_jaxpr/ppermute | solution.py:71
  663.8 14.2 %collective-permute-start.6 = (bf16[512,832]{0,1:T(8,128)(2,1)}, bf16[512,832]{0,1:T(8,128)(2,1)}, u32[]{:S(2)}, u32[]{:S(2)}) collective-permute-start(bf16[512,832]{0,1:T(8,128)(2,1)} %collective-permute-done.5), channel_id=1, source_target_pairs={{0,1},{1,2},{2,3},{3,4},{4,5},{5,6},{6,7},{7,0},{8,9},{9,10},{10,1... | collective-permute-start | bytes 2555912 | tf_op jit(solution)/shard_map/while/body/eval_jaxpr/ppermute | solution.py:71
  699.3 18.4 %collective-permute-start.7 = (bf16[512,832]{0,1:T(8,128)(2,1)S(1)}, bf16[512,832]{0,1:T(8,128)(2,1)}, u32[]{:S(2)}, u32[]{:S(2)}) collective-permute-start(bf16[512,832]{0,1:T(8,128)(2,1)S(1)} %get-tuple-element.370), channel_id=1, source_target_pairs={{8,0},{16,8},{24,16},{9,1},{17,9},{25,17},{10,2},{18,10},{26,18},{... | collective-permute-start | bytes 2555912 | tf_op jit(solution)/shard_map/while/body/eval_jaxpr/ppermute | solution.py:14
  (45 other events, 692.6 us)
Sparse Core Ops, SparseCore 0:
  10.2 28.7 all-gather.1
  102.3 40.6 reduce-scatter.3
